TPU v7x, 256 devices: a whole 4x4x8 slice. The times are simulated.
256 devices in a mesh: ep: 64 (over z, x, core), tp: 4 (over y).
Axes of the slice: x: 4, y: 4, z: 8, core: 2. Of those that a mesh axis runs over, the one named last changes fastest.
Arguments:
- tokens: bfloat16 [16384, 3584], P('ep', 'tp'), may hold values from -6 to 6
- grad_out: bfloat16 [16384, 3584], P('ep', 'tp'), may hold values from -6 to 6
- route_ids: int32 [16384, 2], P('ep'), may hold values from 0 to 63, all different within a row; in each aligned block of 256 rows (0 to 255, 256 to 511, ...) at most 16 rows name the same one
- route_probs: float32 [16384, 2], P('ep'), may hold values from 0.2 to 1
- w_gate: bfloat16 [64, 3584, 1024], P('ep', None, 'tp'), may hold values from -0.09375 to 0.09375
- w_up: bfloat16 [64, 3584, 1024], P('ep', None, 'tp'), may hold values from -0.09375 to 0.09375
- w_down: bfloat16 [64, 1024, 3584], P('ep', 'tp'), may hold values from -0.1875 to 0.1875
Outputs:
- grad_tokens: bfloat16 [16384, 3584], P('ep', 'tp')
- grad_gate: bfloat16 [64, 3584, 1024], P('ep', None, 'tp')
- grad_up: bfloat16 [64, 3584, 1024], P('ep', None, 'tp')
- grad_down: bfloat16 [64, 1024, 3584], P('ep', 'tp')
Inputs may be any that keep to these rules, and one draw needn't show every extreme that they name: `route_ids`: each token names 2 different experts. Among the tokens of one index of ep (aligned blocks of 256 tokens), no expert is named by more than 16 tokens, and in every draw some expert is named by exactly 16 of some block.
All inputs are finite; a program needn't handle non-finite values.
Results may differ from a plain program's by a relative error of at most 0.0065.
Values may be sent and summed in bfloat16 or wider, within the bound.
No kernel may reach another device: no remote copies, remote signals or barrier semaphores. Data moves between devices by JAX's collectives and lax.ppermute only.
A program may use at most 128 MiB of HBM per device.

v0:
```python
import jax
import jax.numpy as jnp
from jax import lax
from jax.sharding import PartitionSpec as P


def contract_last(left, right):
    return lax.dot_general(
        left, right, (((1,), (1,)), ((), ())), preferred_element_type=jnp.float32
    )


def contract_first(left, right):
    return lax.dot_general(
        left, right, (((0,), (0,)), ((), ())), preferred_element_type=jnp.float32
    )


def row_pass(x_rows, s_rows, gate_cols, up_cols, down_rows):
    gate = jnp.dot(x_rows, gate_cols, preferred_element_type=jnp.float32)
    upper = jnp.dot(x_rows, up_cols, preferred_element_type=jnp.float32)
    sigma = jax.nn.sigmoid(gate)
    active = gate * sigma
    hidden = (active * upper).astype(jnp.bfloat16)
    back = contract_last(s_rows, down_rows)
    d_up = (back * active).astype(jnp.bfloat16)
    d_gate = (back * upper * sigma * (1.0 + gate * (1.0 - sigma))).astype(jnp.bfloat16)
    return (
        d_gate,
        d_up,
        contract_first(x_rows, d_gate),
        contract_first(x_rows, d_up),
        contract_first(hidden, s_rows),
    )


def per_device(tokens, grad_out, route_ids, route_probs, w_gate, w_up, w_down):
    n_src = lax.axis_size("ep")
    tok_rows, quarter = tokens.shape
    top = route_ids.shape[1]
    width = w_gate.shape[1]
    cap = max(2, 2 * tok_rows * top // n_src)
    total_rows = n_src * cap
    gate_cols = w_gate[0]
    up_cols = w_up[0]
    down_rows = w_down[0]
    flat_ids = route_ids.reshape(-1)
    routes = flat_ids.shape[0]
    onehot = (flat_ids[:, None] == jnp.arange(n_src, dtype=jnp.int32)[None, :]).astype(jnp.int32)
    rank = jnp.sum((jnp.cumsum(onehot, axis=0) - onehot) * onehot, axis=1)
    slot = flat_ids * cap + rank
    route_of = (
        jnp.full((n_src * cap,), routes, jnp.int32)
        .at[slot]
        .set(jnp.arange(routes, dtype=jnp.int32))
    )
    filled = route_of < routes
    token_of = jnp.where(filled, route_of // top, tok_rows)
    x_send = jnp.take(tokens, token_of, axis=0, mode="fill", fill_value=0).reshape(
        n_src, cap, quarter
    )
    scaled = (route_probs[:, :, None] * grad_out[:, None, :].astype(jnp.float32)).astype(
        jnp.bfloat16
    )
    s_send = jnp.take(
        scaled.reshape(routes, quarter), route_of, axis=0, mode="fill", fill_value=0
    ).reshape(n_src, cap, quarter)
    x_recv, s_recv = (
        lax.all_to_all(x_send, "ep", split_axis=0, concat_axis=0, tiled=True),
        lax.all_to_all(s_send, "ep", split_axis=0, concat_axis=0, tiled=True),
    )
    x_full, s_full = (
        lax.all_gather(x_recv, "tp", axis=2, tiled=True),
        lax.all_gather(s_recv, "tp", axis=2, tiled=True),
    )
    x_rows = x_full.reshape(total_rows, width)
    s_rows = s_full.reshape(total_rows, width)
    d_gate, d_up, g_gate, g_up, g_down = row_pass(x_rows, s_rows, gate_cols, up_cols, down_rows)
    part = contract_last(d_gate, gate_cols) + contract_last(d_up, up_cols)
    dx_rows = lax.psum_scatter(part, "tp", scatter_dimension=1, tiled=True)
    dx_rows = dx_rows.astype(jnp.bfloat16)
    back_slots = lax.all_to_all(
        dx_rows.reshape(n_src, cap, quarter), "ep", split_axis=0, concat_axis=0, tiled=True
    )
    per_route = jnp.take(back_slots.reshape(n_src * cap, quarter), slot, axis=0)
    grad_tokens = jnp.sum(
        per_route.reshape(tok_rows, top, quarter).astype(jnp.float32), axis=1
    ).astype(jnp.bfloat16)
    return (
        grad_tokens,
        g_gate.astype(jnp.bfloat16)[None],
        g_up.astype(jnp.bfloat16)[None],
        g_down.astype(jnp.bfloat16)[None],
    )


def solution(mesh):
    placed = (
        P("ep", "tp"),
        P("ep", "tp"),
        P("ep", None),
        P("ep", None),
        P("ep", None, "tp"),
        P("ep", None, "tp"),
        P("ep", "tp", None),
    )
    return jax.shard_map(
        per_device,
        mesh=mesh,
        in_specs=placed,
        out_specs=(P("ep", "tp"), P("ep", None, "tp"), P("ep", None, "tp"), P("ep", "tp", None)),
        check_vma=False,
    )
```

profile of v0, /device:TPU:2, one launch (start us, length us, event | category | flops | bytes accessed | tf_op | source)
XLA Modules:
  0.0 459.1 jit_solution(468386669442834185)
XLA Ops:
  7.2 0.0 all-gather.5.cloned.1.call-start
  7.2 0.9 broadcast_multiply_fusion
  8.1 0.8 copy.17
  8.9 0.1 eq.26
  9.1 0.1 reshape.113
  9.2 0.1 copy.22
  9.3 0.1 mul.64
  9.5 1.2 reduce-window.6
  10.7 0.2 slice_reduce_fusion
  11.0 0.1 fusion.17
  11.1 2.4 scatter_custom_fusion
  13.6 0.1 broadcast_in_dim.59
  13.7 5.3 %gather_fusion.1 = bf16[1024,896]{1,0:T(8,128)(2,1)} fusion(bf16[256,896]{1,0:T(8,128)(2,1)S(1)} %copy-done.2, s32[1024]{0:T(1024)S(1)} %get-tuple-element.9), kind=kCustom, calls=%fused_computation.1 | custom fusion | bytes 3674112 | tf_op jit(solution)/shard_map/jit(_take)/gather | solution.py:59
  19.0 1.8 broadcast_select_fusion
  20.8 57.5 %all_to_all.15 = bf16[64,16,896]{2,1,0:T(8,128)(2,1)} all-to-all(bf16[64,16,896]{2,1,0:T(8,128)(2,1)S(1)} %broadcast_select_fusion), channel_id=1, replica_groups=mesh['ep'=64,'tp'=4] {'ep'}, dimensions={0} | all-to-all | bytes 3670016 | tf_op jit(solution)/shard_map/all_to_all | solution.py:69
  78.4 0.0 all-gather.3.cloned.1.call-start
  78.4 0.1 broadcast_in_dim.54
  78.5 0.5 copy-done.7
  79.0 0.1 copy.23
  79.2 0.1 mul.65
  79.3 0.1 copy-done.5
  79.4 1.7 mul.67
  81.1 3.4 mul.68
  84.5 1.7 multiply_convert_fusion
  86.1 5.3 %gather_fusion = bf16[1024,896]{1,0:T(8,128)(2,1)} fusion(bf16[512,896]{1,0:T(8,128)(2,1)S(1)} %multiply_convert_fusion, s32[1024]{0:T(1024)S(1)} %get-tuple-element.8), kind=kCustom, calls=%fused_computation | custom fusion | bytes 3674112 | tf_op jit(solution)/shard_map/jit(_take)/gather | solution.py:65
  91.4 1.9 broadcast_select_fusion.1
  93.3 51.0 %all_to_all.16 = bf16[64,16,896]{2,1,0:T(8,128)(2,1)} all-to-all(bf16[64,16,896]{2,1,0:T(8,128)(2,1)S(1)} %broadcast_select_fusion.1), channel_id=1, replica_groups=mesh['ep'=64,'tp'=4] {'ep'}, dimensions={0} | all-to-all | bytes 3670016 | tf_op jit(solution)/shard_map/all_to_all | solution.py:70
  144.4 0.2 reduce-scatter.2.cloned.1.call-start
  144.6 7.2 %all-gather.5.cloned.1.call-done = bf16[64,16,3584]{2,1,0:T(8,128)(2,1)} async-done(((bf16[64,16,896]{2,1,0:T(8,128)(2,1)}), bf16[64,16,3584]{2,1,0:T(8,128)(2,1)}) %all-gather.5.cloned.1.call-update) | async-done | bytes 7340048 | tf_op jit(solution)/shard_map/all_gather | solution.py:73
  151.8 6.3 %fusion.5 = f32[1024,256]{1,0:T(8,128)} fusion(bf16[1024,3584]{1,0:T(8,128)(2,1)} %bitcast.64, bf16[1,3584,256]{2,1,0:T(8,128)(2,1)S(1)} %copy-done), kind=kOutput, calls=%fused_computation.13 | convolution fusion | flops 1879048192 | bytes 10223616 | tf_op jit(solution)/shard_map/dot_general | solution.py:20
  158.1 3.1 fusion.8
  161.1 70.3 %all-gather.3.cloned.1.call-done = bf16[64,16,3584]{2,1,0:T(8,128)(2,1)} async-done(((bf16[64,16,896]{2,1,0:T(8,128)(2,1)}), bf16[64,16,3584]{2,1,0:T(8,128)(2,1)}) %all-gather.3.cloned.1.call-update) | async-done | bytes 7340048 | tf_op jit(solution)/shard_map/all_gather | solution.py:74
  231.4 6.4 %multiply_convert_fusion.2 = (bf16[1024,256]{1,0:T(8,128)(2,1)S(1)}, bf16[1024,256]{1,0:T(8,128)(2,1)S(1)}) fusion(f32[1024,256]{1,0:T(8,128)} %fusion.5, f32[1024,256]{1,0:T(8,128)} %fusion.8, bf16[1024,3584]{1,0:T(8,128)(2,1)} %bitcast.68, bf16[1,256,3584]{2,1,0:T(8,128)(2,1)} %param.13), kind=kOutput, calls=%fused_computation.25 | convolution fusion | flops 1882456064 | bytes 12320768 | tf_op jit(solution)/shard_map/dot_general | solution.py:8
  237.8 2.1 fusion.3
  240.0 7.6 %convolution_add_fusion = f32[1024,3584]{1,0:T(8,128)} fusion(f32[1024,3584]{1,0:T(8,128)S(1)} %fusion.3, bf16[1024,256]{1,0:T(8,128)(2,1)S(1)} %get-tuple-element.4, bf16[1,3584,256]{2,1,0:T(8,128)(2,1)S(1)} %copy-done.4), kind=kOutput, calls=%fused_computation.4 | convolution fusion | flops 1882718208 | bytes 31719424 | tf_op jit(solution)/shard_map/dot_general | solution.py:8
  247.6 135.1 %reduce-scatter.2.cloned.1.call-done = f32[1024,896]{1,0:T(8,128)} async-done(((f32[1024,3584]{1,0:T(8,128)}), f32[1024,896]{1,0:T(8,128)}) %reduce-scatter.2.cloned.1.call-update) | async-done | bytes 3670032 | tf_op jit(solution)/shard_map/reduce_scatter | solution.py:80
  382.7 3.5 convert_element_type.44
  386.2 10.9 %all-to-all-start.2 = ((bf16[64,16,896]{2,1,0:T(8,128)(2,1)}), bf16[64,16,896]{2,1,0:T(8,128)(2,1)}, u32[]{:S(2)}, u32[]{:S(2)}) async-start(bf16[64,16,896]{2,1,0:T(8,128)(2,1)} %bitcast.10), calls=%async_computation.3 | async-start | bytes 3670016 | tf_op jit(solution)/shard_map/all_to_all | solution.py:82
  397.0 0.1 reduce_sum.26
  397.2 0.1 copy.20
  397.3 0.2 copy.21
  397.5 6.6 %fusion.1 = bf16[1,3584,256]{2,1,0:T(8,128)(2,1)} fusion(bf16[1024,3584]{1,0:T(8,128)(2,1)} %bitcast.65, bf16[1024,256]{1,0:T(8,128)(2,1)S(1)} %get-tuple-element.4), kind=kOutput, calls=%fused_computation.9 | convolution fusion | flops 1879965696 | bytes 9699328 | tf_op jit(solution)/shard_map/dot_general | solution.py:14
  404.1 6.6 %fusion = bf16[1,3584,256]{2,1,0:T(8,128)(2,1)} fusion(bf16[1024,3584]{1,0:T(8,128)(2,1)} %bitcast.66, bf16[1024,256]{1,0:T(8,128)(2,1)S(1)} %get-tuple-element.5), kind=kOutput, calls=%fused_computation.8 | convolution fusion | flops 1879965696 | bytes 9699328 | tf_op jit(solution)/shard_map/dot_general | solution.py:14
  410.7 3.4 fusion.2
  414.1 28.5 %all-to-all-done.2 = bf16[64,16,896]{2,1,0:T(8,128)(2,1)} async-done(((bf16[64,16,896]{2,1,0:T(8,128)(2,1)}), bf16[64,16,896]{2,1,0:T(8,128)(2,1)}, u32[]{:S(2)}, u32[]{:S(2)}) %all-to-all-start.2) | async-done | bytes 1835040 | tf_op jit(solution)/shard_map/all_to_all | solution.py:82
  442.6 4.4 gather_fusion.2
  447.0 1.3 gather.23
  448.3 4.3 fusion.13
  (37 shorter events, 0.2 us)
Async XLA Ops:
  7.2 144.6 %copy-start = (bf16[1,3584,256]{2,1,0:T(8,128)(2,1)S(1)}, bf16[1,3584,256]{2,1,0:T(8,128)(2,1)}, u32[]{:S(2)}) copy-start(bf16[1,3584,256]{2,1,0:T(8,128)(2,1)} %param.11) | copy-start | bytes 5505028
  7.2 6.5 %copy-start.2 = (bf16[256,896]{1,0:T(8,128)(2,1)S(1)}, bf16[256,896]{1,0:T(8,128)(2,1)}, u32[]{:S(2)}) copy-start(bf16[256,896]{1,0:T(8,128)(2,1)} %param.7) | copy-start | bytes 1376260
  7.2 144.6 %all-gather.5.cloned.1.call-start = ((), (), s32[]{:S(2)}) async-start(), calls=%async_computation.5 | async-start | bytes 9175040 | tf_op jit(solution)/shard_map/all_gather | solution.py:73
  78.3 0.7 copy-start.7
  78.3 1.0 copy-start.5
  78.4 153.0 %all-gather.3.cloned.1.call-start = ((), (), s32[]{:S(2)}) async-start(), calls=%async_computation.4 | async-start | bytes 9175040 | tf_op jit(solution)/shard_map/all_gather | solution.py:74
  144.4 238.3 %reduce-scatter.2.cloned.1.call-start = ((), (), s32[]{:S(2)}) async-start(), calls=%async_computation.6 | async-start | bytes 18350080 | tf_op jit(solution)/shard_map/reduce_scatter | solution.py:80
  151.8 6.3 %copy-start.3 = (bf16[1,3584,256]{2,1,0:T(8,128)(2,1)S(1)}, bf16[1,3584,256]{2,1,0:T(8,128)(2,1)}, u32[]{:S(2)}) copy-start(bf16[1,3584,256]{2,1,0:T(8,128)(2,1)} %param.12) | copy-start | bytes 5505028
  151.8 6.3 %copy-start.8 = (bf16[64,16,3584]{2,1,0:T(8,128)(2,1)S(1)}, bf16[64,16,3584]{2,1,0:T(8,128)(2,1)}, u32[]{:S(2)}) copy-start(bf16[64,16,3584]{2,1,0:T(8,128)(2,1)} %all-gather.5.cloned.1.call-done) | copy-start | bytes 22020100
  237.8 2.1 copy-start.4
  386.2 11.1 %copy-start.6 = (s32[256,2]{0,1:T(2,128)S(1)}, s32[256,2]{0,1:T(2,128)}, u32[]{:S(2)}) copy-start(s32[256,2]{0,1:T(2,128)} %param.9) | copy-start | bytes 6148
  386.2 56.4 %all-to-all-start.2 = ((bf16[64,16,896]{2,1,0:T(8,128)(2,1)}), bf16[64,16,896]{2,1,0:T(8,128)(2,1)}, u32[]{:S(2)}, u32[]{:S(2)}) async-start(bf16[64,16,896]{2,1,0:T(8,128)(2,1)} %bitcast.10), calls=%async_computation.3 | async-start | bytes 3670016 | tf_op jit(solution)/shard_map/all_to_all | solution.py:82
  397.5 13.2 %slice-start = ((s8[7340032]{0:T(1024)(128)(4,1)}), s8[4194304]{0:T(1024)(128)(4,1)S(1)}, s32[]{:S(2)}) async-start(s8[7340032]{0:T(1024)(128)(4,1)} %bitcast.69), calls=%async_computation.7 | async-start | bytes 8388608
  404.1 6.6 %slice-start.1 = ((s8[7340032]{0:T(1024)(128)(4,1)}), s8[3145728]{0:T(1024)(128)(4,1)S(1)}, s32[]{:S(2)}) async-start(s8[7340032]{0:T(1024)(128)(4,1)} %bitcast.69), calls=%async_computation.8 | async-start | bytes 6291456
  404.1 6.6 %copy-start.9 = (f32[1024,256]{1,0:T(8,128)S(1)}, f32[1024,256]{1,0:T(8,128)}, u32[]{:S(2)}) copy-start(f32[1024,256]{1,0:T(8,128)} %fusion.5) | copy-start | bytes 3145732
  404.1 6.6 %copy-start.10 = (f32[1024,256]{1,0:T(8,128)S(1)}, f32[1024,256]{1,0:T(8,128)}, u32[]{:S(2)}) copy-start(f32[1024,256]{1,0:T(8,128)} %fusion.8) | copy-start | bytes 3145732
  442.6 10.0 %copy-start.1 = (bf16[1,3584,256]{2,1,0:T(8,128)(2,1)S(1)}, bf16[1,3584,256]{2,1,0:T(8,128)(2,1)}, u32[]{:S(2)}) copy-start(bf16[1,3584,256]{2,1,0:T(8,128)(2,1)} %param.11) | copy-start | bytes 5505028
Sparse Core Ops, SparseCore 0:
  78.5 73.2 all-gather.4
  153.6 77.7 all-gather.2
  247.7 134.8 reduce-scatter.1
where the time goes:
time: 460 us; the launch traced here: 459 us
  waiting for transfers between devices  241 us (52%)
  blocking collectives  109 us (24%)
  matrix products  42 us (9%)
  local copies, waits for them, and re-layouts  26.8 us (6%)
  other arithmetic  15.5 us (3%)
  between operations  14 us (3%)
  starting transfers between devices  11.2 us (2%)
    reduce_scatter x1, waiting for transfers between devices, per_device(): dx_rows = lax.psum_scatter(part, 'tp', scatter_dimension=1, tiled=True)  135 us
    all_gather x1, waiting for transfers between devices, per_device(): lax.all_gather(s_recv, 'tp', axis=2, tiled=True)  70.3 us
    all_to_all x1, blocking collectives, per_device(): lax.all_to_all(x_send, 'ep', split_axis=0, concat_axis=0, tiled=True)  57.5 us
    all_to_all x1, blocking collectives, per_device(): lax.all_to_all(s_send, 'ep', split_axis=0, concat_axis=0, tiled=True)  51 us
    all_to_all x1, waiting for transfers between devices, per_device(): lax.all_to_all(dx_rows.reshape(n_src, cap, quarter), 'ep', split_axis=0,...  28.5 us
    dot_general x3, matrix products, contract_first(): lax.dot_general(left, right, (((0,), (0,)), ((), ())), preferred_element_...  16.6 us
    dot_general x3, matrix products, contract_last(): lax.dot_general(left, right, (((1,), (1,)), ((), ())), preferred_element_...  16.2 us
    all_to_all x1, starting transfers between devices, per_device(): lax.all_to_all(dx_rows.reshape(n_src, cap, quarter), 'ep', split_axis=0,...  10.9 us
  transfers between devices with their start and end apart: 4, of which 4 were waited for; matrix products, arithmetic and copies ran while one was open for 9% of the time, Pallas kernels for 0%

commit v1 on v0

--- a/solution.py
+++ b/solution.py
@@ -71,7 +71,9 @@
     )
     x_full, s_full = (
         lax.all_gather(x_recv, "tp", axis=2, tiled=True),
-        lax.all_gather(s_recv, "tp", axis=2, tiled=True),
+        jnp.concatenate(
+            lax.all_to_all(jnp.stack([s_recv] * lax.axis_size("tp")), "tp", 0, 0), axis=2
+        ),
     )
     x_rows = x_full.reshape(total_rows, width)
     s_rows = s_full.reshape(total_rows, width)

time: 460 us -> 493 us (1.072); the launches traced: 459 us -> 486 us
  blocking collectives: 109 us -> 194 us
  waiting for transfers between devices: 241 us -> 163 us
  local copies, waits for them, and re-layouts: 26.8 us -> 51.4 us
  matrix products: 42 us -> 36 us
    all_to_all x0 -> x1, blocking collectives: none -> 85.7 us  [per_device(): lax.all_to_all(jnp.stack([s_recv] * lax.axis_size('tp')), 'tp', 0, 0)]
    all_gather x1 -> x0, waiting for transfers between devices: 70.3 us -> none  [per_device(): lax.all_gather(s_recv, 'tp', axis=2, tiled=True)]
    reshape x0 -> x1, local copies, waits for them, and re-layouts: none -> 15.5 us  [per_device(): jnp.concatenate(lax.all_to_all(jnp.stack([s_recv] * lax.axis_size('tp')),...]
    unnamed x28 -> x37, local copies, waits for them, and re-layouts: 1.58 us -> 10.2 us
    all_gather x1, waiting for transfers between devices: 7.21 us -> 0.01 us  [per_device(): lax.all_gather(x_recv, 'tp', axis=2, tiled=True)]
  transfers between devices with their start and end apart: 4 -> 3, of which waited for: 4 -> 2; matrix products, arithmetic and copies ran while one was open for 9% -> 11% of each run, Pallas kernels for 0% -> 0%
where the time goes in v1:
time: 493 us; the launch traced here: 486 us
  blocking collectives  194 us (39%)
  waiting for transfers between devices  163 us (33%)
  local copies, waits for them, and re-layouts  51.4 us (10%)
  matrix products  36 us (7%)
  other arithmetic  15.5 us (3%)
  between operations  14.6 us (3%)
  starting transfers between devices  11.3 us (2%)
    reduce_scatter x1, waiting for transfers between devices, per_device(): dx_rows = lax.psum_scatter(part, 'tp', scatter_dimension=1, tiled=True)  135 us
    all_to_all x1, blocking collectives, per_device(): lax.all_to_all(jnp.stack([s_recv] * lax.axis_size('tp')), 'tp', 0, 0)  85.7 us
    all_to_all x1, blocking collectives, per_device(): lax.all_to_all(x_send, 'ep', split_axis=0, concat_axis=0, tiled=True)  57.5 us
    all_to_all x1, blocking collectives, per_device(): lax.all_to_all(s_send, 'ep', split_axis=0, concat_axis=0, tiled=True)  50.9 us
    all_to_all x1, waiting for transfers between devices, per_device(): lax.all_to_all(dx_rows.reshape(n_src, cap, quarter), 'ep', split_axis=0,...  28.3 us
    dot_general x3, matrix products, contract_first(): lax.dot_general(left, right, (((0,), (0,)), ((), ())), preferred_element_...  16.5 us
    reshape x1, local copies, waits for them, and re-layouts, per_device(): jnp.concatenate(lax.all_to_all(jnp.stack([s_recv] * lax.axis_size('tp')),...  15.5 us
    dot_general x3, matrix products, contract_last(): lax.dot_general(left, right, (((1,), (1,)), ((), ())), preferred_element_...  12 us
  transfers between devices with their start and end apart: 3, of which 2 were waited for; matrix products, arithmetic and copies ran while one was open for 11% of the time, Pallas kernels for 0%

profile of v1, /device:TPU:2, one launch (start us, length us, event | category | flops | bytes accessed | tf_op | source)
XLA Modules:
  0.0 486.0 jit_solution(2356060741169689674)
XLA Ops:
  7.2 0.9 broadcast_multiply_fusion
  8.1 0.8 copy.23
  8.9 0.1 eq.26
  9.1 0.1 reshape.115
  9.2 0.1 copy.28
  9.3 0.1 mul.64
  9.5 1.2 reduce-window.6
  10.7 0.2 slice_reduce_fusion
  11.0 0.1 fusion.17
  11.1 2.4 scatter_custom_fusion
  13.6 0.1 broadcast_in_dim.59
  13.7 5.3 %gather_fusion.1 = bf16[1024,896]{1,0:T(8,128)(2,1)} fusion(bf16[256,896]{1,0:T(8,128)(2,1)S(1)} %copy-done.2, s32[1024]{0:T(1024)S(1)} %get-tuple-element.9), kind=kCustom, calls=%fused_computation.1 | custom fusion | bytes 3674112 | tf_op jit(solution)/shard_map/jit(_take)/gather | solution.py:59
  19.0 1.8 broadcast_select_fusion
  20.8 57.5 %all_to_all.20 = bf16[64,16,896]{2,1,0:T(8,128)(2,1)} all-to-all(bf16[64,16,896]{2,1,0:T(8,128)(2,1)S(1)} %broadcast_select_fusion), channel_id=1, replica_groups=mesh['ep'=64,'tp'=4] {'ep'}, dimensions={0} | all-to-all | bytes 3670016 | tf_op jit(solution)/shard_map/all_to_all | solution.py:69
  78.4 0.1 broadcast_in_dim.54
  78.5 0.5 copy-done.6
  79.0 0.1 copy.29
  79.2 0.1 mul.65
  79.4 1.7 mul.67
  81.1 3.4 mul.68
  84.5 1.7 multiply_convert_fusion
  86.1 5.3 %gather_fusion = bf16[1024,896]{1,0:T(8,128)(2,1)} fusion(bf16[512,896]{1,0:T(8,128)(2,1)S(1)} %multiply_convert_fusion, s32[1024]{0:T(1024)S(1)} %get-tuple-element.8), kind=kCustom, calls=%fused_computation | custom fusion | bytes 3674112 | tf_op jit(solution)/shard_map/jit(_take)/gather | solution.py:65
  91.4 1.9 broadcast_select_fusion.1
  93.3 50.9 %all_to_all.21 = bf16[64,16,896]{2,1,0:T(8,128)(2,1)S(1)} all-to-all(bf16[64,16,896]{2,1,0:T(8,128)(2,1)S(1)} %broadcast_select_fusion.1), channel_id=1, replica_groups=mesh['ep'=64,'tp'=4] {'ep'}, dimensions={0} | all-to-all | bytes 3670016 | tf_op jit(solution)/shard_map/all_to_all | solution.py:70
  144.2 0.5 stack.2
  144.8 85.7 %all_to_all.22 = bf16[4,64,16,896]{3,2,1,0:T(8,128)(2,1)} all-to-all(bf16[4,64,16,896]{3,2,1,0:T(8,128)(2,1)S(1)} %stack.2), channel_id=1, replica_groups=mesh['ep'=64,'tp'=4] {'tp'}, dimensions={0} | all-to-all | bytes 14680064 | tf_op jit(solution)/shard_map/all_to_all | solution.py:75
  230.5 15.5 %copy.30 = bf16[64,16,4,896]{3,2,1,0:T(4,128)(2,1)} copy(bf16[64,16,4,896]{3,1,0,2:T(8,128)(2,1)} %bitcast.62) | data formatting | bytes 14680064 | tf_op jit(solution)/shard_map/reshape | solution.py:74
  245.9 7.3 %copy.32 = bf16[128,8,4,896]{3,1,2,0:T(8,128)(2,1)} copy(bf16[128,8,4,896]{3,2,1,0:T(4,128)(2,1)} %bitcast.63) | data formatting | bytes 14680064
  253.3 5.5 %fusion.5 = f32[1024,256]{1,0:T(8,128)S(1)} fusion(bf16[1024,3584]{1,0:T(8,128)(2,1)} %bitcast.75, bf16[1,3584,256]{2,1,0:T(8,128)(2,1)S(1)} %copy-done), kind=kOutput, calls=%fused_computation.13 | convolution fusion | flops 1879048192 | bytes 10223616 | tf_op jit(solution)/shard_map/dot_general | solution.py:20
  258.7 0.2 copy-done.7
  259.0 2.1 fusion.8
  261.1 0.5 slice-done.1
  261.6 0.5 copy-done.8
  262.1 2.3 multiply_convert_fusion.2
  264.4 2.1 fusion.3
  266.5 7.6 %convolution_add_fusion = f32[1024,3584]{1,0:T(8,128)} fusion(f32[1024,3584]{1,0:T(8,128)S(1)} %fusion.3, bf16[1024,256]{1,0:T(8,128)(2,1)S(1)} %get-tuple-element.4, bf16[1,3584,256]{2,1,0:T(8,128)(2,1)S(1)} %copy-done.3), kind=kOutput, calls=%fused_computation.4 | convolution fusion | flops 1882718208 | bytes 31719424 | tf_op jit(solution)/shard_map/dot_general | solution.py:8
  274.1 134.8 %reduce-scatter.2.cloned.1.call-done = f32[1024,896]{1,0:T(8,128)} async-done(((f32[1024,3584]{1,0:T(8,128)}), f32[1024,896]{1,0:T(8,128)}) %reduce-scatter.2.cloned.1.call-update) | async-done | bytes 3670032 | tf_op jit(solution)/shard_map/reduce_scatter | solution.py:82
  408.9 3.5 convert_element_type.44
  412.4 11.2 %all-to-all-start.3 = ((bf16[64,16,896]{2,1,0:T(8,128)(2,1)}), bf16[64,16,896]{2,1,0:T(8,128)(2,1)}, u32[]{:S(2)}, u32[]{:S(2)}) async-start(bf16[64,16,896]{2,1,0:T(8,128)(2,1)} %bitcast.10), calls=%async_computation.4 | async-start | bytes 3670016 | tf_op jit(solution)/shard_map/all_to_all | solution.py:84
  423.6 0.1 reduce_sum.26
  423.8 0.2 copy.27
  424.0 6.6 %fusion.1 = bf16[1,3584,256]{2,1,0:T(8,128)(2,1)} fusion(bf16[1024,3584]{1,0:T(8,128)(2,1)} %bitcast.76, bf16[1024,256]{1,0:T(8,128)(2,1)S(1)} %get-tuple-element.4), kind=kOutput, calls=%fused_computation.9 | convolution fusion | flops 1879965696 | bytes 9699328 | tf_op jit(solution)/shard_map/dot_general | solution.py:14
  430.6 6.6 %fusion = bf16[1,3584,256]{2,1,0:T(8,128)(2,1)} fusion(bf16[1024,3584]{1,0:T(8,128)(2,1)} %bitcast.77, bf16[1024,256]{1,0:T(8,128)(2,1)S(1)} %get-tuple-element.5), kind=kOutput, calls=%fused_computation.8 | convolution fusion | flops 1879965696 | bytes 9699328 | tf_op jit(solution)/shard_map/dot_general | solution.py:14
  437.3 3.4 fusion.2
  440.6 28.3 %all-to-all-done.3 = bf16[64,16,896]{2,1,0:T(8,128)(2,1)} async-done(((bf16[64,16,896]{2,1,0:T(8,128)(2,1)}), bf16[64,16,896]{2,1,0:T(8,128)(2,1)}, u32[]{:S(2)}, u32[]{:S(2)}) %all-to-all-start.3) | async-done | bytes 1835040 | tf_op jit(solution)/shard_map/all_to_all | solution.py:84
  469.0 4.4 gather_fusion.2
  473.4 1.3 gather.23
  474.6 4.3 fusion.13
  (47 shorter events, 0.4 us)
Async XLA Ops:
  7.2 246.1 %copy-start = (bf16[1,3584,256]{2,1,0:T(8,128)(2,1)S(1)}, bf16[1,3584,256]{2,1,0:T(8,128)(2,1)}, u32[]{:S(2)}) copy-start(bf16[1,3584,256]{2,1,0:T(8,128)(2,1)} %param.11) | copy-start | bytes 5505028
  7.2 6.5 %copy-start.2 = (bf16[256,896]{1,0:T(8,128)(2,1)S(1)}, bf16[256,896]{1,0:T(8,128)(2,1)}, u32[]{:S(2)}) copy-start(bf16[256,896]{1,0:T(8,128)(2,1)} %param.7) | copy-start | bytes 1376260
  7.2 246.1 %all-gather.2.cloned.1.call-start = ((), (), s32[]{:S(2)}) async-start(), calls=%async_computation.5 | async-start | bytes 9175040 | tf_op jit(solution)/shard_map/all_gather | solution.py:73
  78.3 0.7 copy-start.6
  78.3 1.0 copy-start.4
  78.4 330.5 %reduce-scatter.2.cloned.1.call-start = ((), (), s32[]{:S(2)}) async-start(), calls=%async_computation.6 | async-start | bytes 18350080 | tf_op jit(solution)/shard_map/reduce_scatter | solution.py:82
  253.2 5.5 %copy-start.3 = (bf16[1,3584,256]{2,1,0:T(8,128)(2,1)S(1)}, bf16[1,3584,256]{2,1,0:T(8,128)(2,1)}, u32[]{:S(2)}) copy-start(bf16[1,3584,256]{2,1,0:T(8,128)(2,1)} %param.12) | copy-start | bytes 5505028
  253.3 5.7 %copy-start.7 = (bf16[64,16,3584]{2,1,0:T(8,128)(2,1)S(1)}, bf16[64,16,3584]{2,1,0:T(8,128)(2,1)}, u32[]{:S(2)}) copy-start(bf16[64,16,3584]{2,1,0:T(8,128)(2,1)} %all-gather.2.cloned.1.call-done) | copy-start | bytes 22020100
  253.3 7.8 %slice-start = ((s8[7340032]{0:T(1024)(128)(4,1)}), s8[4194304]{0:T(1024)(128)(4,1)S(1)}, s32[]{:S(2)}) async-start(s8[7340032]{0:T(1024)(128)(4,1)} %bitcast.66), calls=%async_computation.7 | async-start | bytes 8388608
  259.0 2.1 copy-start.9
  259.0 2.6 slice-start.1
  259.0 3.1 copy-start.8
  261.1 3.3 copy-start.11
  412.4 11.5 %copy-start.5 = (s32[256,2]{0,1:T(2,128)S(1)}, s32[256,2]{0,1:T(2,128)}, u32[]{:S(2)}) copy-start(s32[256,2]{0,1:T(2,128)} %param.9) | copy-start | bytes 6148
  412.4 56.6 %all-to-all-start.3 = ((bf16[64,16,896]{2,1,0:T(8,128)(2,1)}), bf16[64,16,896]{2,1,0:T(8,128)(2,1)}, u32[]{:S(2)}, u32[]{:S(2)}) async-start(bf16[64,16,896]{2,1,0:T(8,128)(2,1)} %bitcast.10), calls=%async_computation.4 | async-start | bytes 3670016 | tf_op jit(solution)/shard_map/all_to_all | solution.py:84
  424.0 13.2 %slice-start.2 = ((s8[7340032]{0:T(1024)(128)(4,1)}), s8[4194304]{0:T(1024)(128)(4,1)S(1)}, s32[]{:S(2)}) async-start(s8[7340032]{0:T(1024)(128)(4,1)} %bitcast.69), calls=%async_computation.9 | async-start | bytes 8388608
  430.6 6.6 %slice-start.3 = ((s8[7340032]{0:T(1024)(128)(4,1)}), s8[3145728]{0:T(1024)(128)(4,1)S(1)}, s32[]{:S(2)}) async-start(s8[7340032]{0:T(1024)(128)(4,1)} %bitcast.69), calls=%async_computation.10 | async-start | bytes 6291456
  430.6 6.6 %copy-start.10 = (f32[1024,256]{1,0:T(8,128)S(1)}, f32[1024,256]{1,0:T(8,128)}, u32[]{:S(2)}) copy-start(f32[1024,256]{1,0:T(8,128)} %copy-done.9) | copy-start | bytes 3145732
  430.6 6.6 %copy-start.12 = (f32[1024,256]{1,0:T(8,128)S(1)}, f32[1024,256]{1,0:T(8,128)}, u32[]{:S(2)}) copy-start(f32[1024,256]{1,0:T(8,128)} %copy-done.11) | copy-start | bytes 3145732
  469.0 10.0 %copy-start.1 = (bf16[1,3584,256]{2,1,0:T(8,128)(2,1)S(1)}, bf16[1,3584,256]{2,1,0:T(8,128)(2,1)}, u32[]{:S(2)}) copy-start(bf16[1,3584,256]{2,1,0:T(8,128)(2,1)} %param.11) | copy-start | bytes 5505028
Sparse Core Ops, SparseCore 0:
  78.5 73.8 all-gather.1
  274.3 134.5 reduce-scatter.1
